TPU v7x, 32 devices: a whole 2x2x4 slice. The times are simulated.
32 devices in a mesh: row: 8 (over z, x), col: 4 (over y, core).
Axes of the slice: x: 2, y: 2, z: 4, core: 2. Of those that a mesh axis runs over, the one named last changes fastest.
Arguments:
- features: float32 [136, 8192], P(None, 'row'), may hold values from -6 to 6
- factor: float32 [8192, 16384], P('row', 'col')
Outputs:
- panel: float32 [8192, 512], P(('row', 'col'))
All inputs are finite; a program needn't handle non-finite values.
Results may differ from a plain program's by a relative error of at most 0.000067.
Values sent between devices are 32-bit elements; how exact they have to be, the bound alone decides.
No kernel may reach another device: no remote copies, remote signals or barrier semaphores. Data moves between devices by JAX's collectives and lax.ppermute only.
A program may use at most 128 MiB of HBM per device.

v0:
```python
import jax
import jax.numpy as jnp
from jax import lax
from jax.sharding import PartitionSpec as P

B = 512


ridge_value = 40.0


def broadcast(x, axis, root):
    mine = lax.axis_index(axis) == root
    return lax.psum(jnp.where(mine, x, jnp.zeros_like(x)), axis)


def kernel(points, anchors):
    feature_count = points.shape[0]
    products = lax.dot_general(
        points,
        anchors,
        (((0,), (0,)), ((), ())),
        precision=lax.Precision.HIGHEST,
        preferred_element_type=jnp.float32,
    )
    norm_points = jnp.sum(points * points, axis=0)
    norm_anchors = jnp.sum(anchors * anchors, axis=0)
    distance = norm_points[:, None] + norm_anchors[None, :] - 2.0 * products
    return products / feature_count + jnp.exp(-distance / (2.0 * feature_count))


def times_rows(block, pivot_factor):
    return lax.dot_general(
        block,
        pivot_factor,
        (((1,), (1,)), ((), ())),
        precision=lax.Precision.HIGHEST,
        preferred_element_type=jnp.float32,
    )


def on_device(features, factor):
    rows_dev = factor.shape[0]
    slab_rows = rows_dev // lax.axis_size("col")
    col_index = lax.axis_index("col")
    row_index = lax.axis_index("row")
    pivot_factor, pivot_points = (
        broadcast(factor[:B], "row", 0),
        broadcast(features[:, :B], "row", 0),
    )
    own_points = lax.dynamic_slice_in_dim(features, col_index * slab_rows, slab_rows, 1)
    global_rows = row_index * rows_dev + col_index * slab_rows + lax.iota(jnp.int32, slab_rows)
    identity_rows = (global_rows[:, None] == lax.iota(jnp.int32, B)[None, :]).astype(jnp.float32)
    slab_kernel = kernel(own_points, pivot_points) + ridge_value * identity_rows
    local_sums = lax.psum_scatter(
        times_rows(factor, pivot_factor), "col", scatter_dimension=0, tiled=True
    )
    pivot_kernel = kernel(pivot_points, pivot_points) + ridge_value * jnp.eye(B, dtype=jnp.float32)
    gram_sums = lax.psum(times_rows(pivot_factor, pivot_factor), "col")
    lower_factor = jnp.linalg.cholesky(pivot_kernel - gram_sums)
    slab_values = slab_kernel - local_sums
    solved = jax.scipy.linalg.solve_triangular(lower_factor, slab_values.T, lower=True)
    return solved.T


def solution(mesh):
    placed = (P(None, "row"), P("row", "col"))
    return jax.shard_map(
        on_device, mesh=mesh, in_specs=placed, out_specs=P(("row", "col"), None), check_vma=False
    )
```

profile of v0, /device:TPU:0, one launch (start us, length us, event | category | flops | bytes accessed | tf_op | source)
XLA Modules:
  0.0 501.1 jit_solution(18310001285476813310)
XLA Ops:
  6.5 7.7 %slice_select_fusion = f32[512,4096]{1,0:T(8,128)} fusion(f32[1024,4096]{1,0:T(8,128)} %param.3, pred[]{:T(512)S(6)} %eq.20), kind=kLoop, calls=%fused_computation.2 | loop fusion | flops 2097152 | bytes 16777216 | tf_op jit(solution)/shard_map/jit(_where)/select_n | solution.py:14
  14.3 0.7 slice_select_fusion.1
  15.1 280.9 %all-reduce.7.cloned.1.call-done = (f32[512,4096]{1,0:T(8,128)}, f32[136,512]{1,0:T(8,128)}) async-done(((f32[512,4096]{1,0:T(8,128)}, f32[136,512]{1,0:T(8,128)}), (f32[512,4096]{1,0:T(8,128)}, f32[136,512]{1,0:T(8,128)})) %all-reduce.7.cloned.1.call-update) | async-done | bytes 8667152 | tf_op jit(solution)/shard_map/psum | solution.py:14
  296.0 17.2 %fusion.33 = f32[512,512]{0,1:T(8,128)} fusion(f32[512,4096]{1,0:T(8,128)} %get-tuple-element.25), kind=kOutput, calls=%fused_computation.79 | convolution fusion | flops 12884901888 | bytes 9437184 | tf_op jit(solution)/shard_map/dot_general | solution.py:33
  313.3 31.4 %convolution_bitcast_fusion = f32[1024,512]{1,0:T(8,128)} fusion(f32[512,4096]{1,0:T(8,128)} %get-tuple-element.25, f32[1024,4096]{1,0:T(8,128)} %param.3), kind=kOutput, calls=%fused_computation.3 | convolution fusion | flops 25769803776 | bytes 27262976 | tf_op jit(solution)/shard_map/dot_general | solution.py:33
  344.7 4.1 all-reduce.5.cloned.1.call-done
  348.8 2.6 add_subtract_fusion
  352.0 11.7 %cholesky.103 = f32[128,128]{1,0:T(8,128)S(1)} custom-call(f32[128,128]{1,0:T(8,128)S(1)} %cholesky.263), custom_call_target="Cholesky" | custom-call | tf_op jit(solution)/shard_map/jit(cholesky)/cholesky | solution.py:60
  363.7 9.8 %custom-call.31 = f32[1,128,128]{1,2,0:T(8,128)S(1)} custom-call(f32[1,128,128]{2,1,0:T(8,128)S(1)} %get-tuple-element.34), custom_call_target="InvertDiagBlocksLowerTriangular" | custom-call | tf_op jit(solution)/shard_map/jit(cholesky)/cholesky | solution.py:60
  374.5 11.9 %cholesky.215 = f32[128,128]{1,0:T(8,128)S(1)} custom-call(f32[128,128]{1,0:T(8,128)S(1)} %cholesky.267), custom_call_target="Cholesky" | custom-call | tf_op jit(solution)/shard_map/jit(cholesky)/cholesky | solution.py:60
  386.5 9.8 %custom-call.32 = f32[1,128,128]{1,2,0:T(8,128)S(1)} custom-call(f32[1,128,128]{2,1,0:T(8,128)S(1)} %get-tuple-element.32), custom_call_target="InvertDiagBlocksLowerTriangular" | custom-call | tf_op jit(solution)/shard_map/jit(cholesky)/cholesky | solution.py:60
  396.8 0.6 convolution_subtract_fusion.3
  397.4 11.7 %cholesky.236 = f32[128,128]{1,0:T(8,128)S(1)} custom-call(f32[128,128]{1,0:T(8,128)S(1)} %cholesky.272), custom_call_target="Cholesky" | custom-call | tf_op jit(solution)/shard_map/jit(cholesky)/cholesky | solution.py:60
  409.3 9.8 %custom-call.33 = f32[1,128,128]{1,2,0:T(8,128)S(1)} custom-call(f32[1,128,128]{2,1,0:T(8,128)S(1)} %get-tuple-element.30), custom_call_target="InvertDiagBlocksLowerTriangular" | custom-call | tf_op jit(solution)/shard_map/jit(cholesky)/cholesky | solution.py:60
  419.9 12.0 %cholesky.253 = f32[128,128]{1,0:T(8,128)S(1)} custom-call(f32[128,128]{1,0:T(8,128)S(1)} %convolution_subtract_fusion.5), custom_call_target="Cholesky" | custom-call | tf_op jit(solution)/shard_map/jit(cholesky)/cholesky | solution.py:60
  431.9 0.7 compare_reduce_fusion.2
  434.0 0.6 compare_reduce_fusion.1
  435.3 0.6 compare_reduce_fusion
  436.7 11.2 %while.1 = (s32[]{:T(128)}, f32[512,512]{0,1:T(8,128)S(1)}, s32[4,2]{0,1:T(2,128)S(1)}, f32[4,128,128]{2,1,0:T(8,128)}, s32[]{:T(128)}) while((s32[]{:T(128)}, f32[512,512]{0,1:T(8,128)S(1)}, s32[4,2]{0,1:T(2,128)S(1)}, f32[4,128,128]{2,1,0:T(8,128)}, s32[]{:T(128)}) %tuple.24), condition=%wide.while_cond, body=%wide.while_body.sunk | while | flops 2 | bytes 393829 | solution.py:62
  437.4 1.4 dynamic-slice.7
  438.9 0.6 bitcast_dynamic-update-slice_fusion.2
  440.2 1.4 dynamic-slice.7
  441.7 0.6 bitcast_dynamic-update-slice_fusion.2
  443.0 1.4 dynamic-slice.7
  444.5 0.6 bitcast_dynamic-update-slice_fusion.2
  445.8 1.4 dynamic-slice.7
  447.3 0.6 bitcast_dynamic-update-slice_fusion.2
  447.9 40.1 %custom-call.34 = f32[4,128,128]{1,2,0:T(8,128)S(1)} custom-call(f32[4,128,128]{2,1,0:T(8,128)} %get-tuple-element.12), custom_call_target="InvertDiagBlocksLowerTriangular" | custom-call | tf_op jit(solution)/shard_map/jit(_solve_triangular)/triangular_solve | solution.py:62
  488.1 2.0 subtract_bitcast_fusion
  491.1 0.6 convolution_subtract_fusion.2
  492.0 0.8 convolution_subtract_fusion.1
  493.2 1.0 copy.16
  (60 shorter events, 8.1 us)
Async XLA Ops:
  6.5 289.5 %all-reduce.7.cloned.1.call-start = ((), (), s32[]{:S(2)}) async-start(), calls=%async_computation.3 | async-start | bytes 17334272 | tf_op jit(solution)/shard_map/psum | solution.py:14
  6.5 7.7 %copy-start = (f32[136,1024]{1,0:T(8,128)S(1)}, f32[136,1024]{1,0:T(8,128)}, u32[]{:S(2)}) copy-start(f32[136,1024]{1,0:T(8,128)} %param.2) | copy-start | bytes 1671172
  15.0 333.8 %all-reduce.5.cloned.1.call-start = ((), (), s32[]{:S(2)}) async-start(), calls=%async_computation.1 | async-start | bytes 2097152 | tf_op jit(solution)/shard_map/psum | solution.py:59
  313.2 31.4 %copy-start.1 = (f32[136,512]{1,0:T(8,128)S(1)}, f32[136,512]{1,0:T(8,128)}, u32[]{:S(2)}) copy-start(f32[136,512]{1,0:T(8,128)} %get-tuple-element.26) | copy-start | bytes 835588
  313.2 174.8 %reduce-scatter.2.cloned.1.call-start = ((), (), s32[]{:S(2)}) async-start(), calls=%async_computation.2 | async-start | bytes 2621440 | tf_op jit(solution)/shard_map/reduce_scatter | solution.py:55
Sparse Core Ops, SparseCore 0:
  15.1 280.8 all-reduce.6
  313.4 35.3 all-reduce.4
  351.3 31.7 reduce-scatter.1
where the time goes:
time: 510 us; the launch traced here: 501 us
  waiting for transfers between devices  285 us (56%)
  other arithmetic  128 us (25%)
  matrix products  58.5 us (11%)
  between operations  16.5 us (3%)
  local copies, waits for them, and re-layouts  13.1 us (3%)
    psum x1, waiting for transfers between devices, broadcast(): return lax.psum(jnp.where(mine, x, jnp.zeros_like(x)), axis)  281 us
    another operation x14, other arithmetic, on_device(): lower_factor = jnp.linalg.cholesky(pivot_kernel - gram_sums)  78.8 us
    dot_general x2, matrix products, times_rows(): lax.dot_general(block, pivot_factor, (((1,), (1,)), ((), ())), precision=...  48.6 us
    another operation x3, other arithmetic, on_device(): jax.scipy.linalg.solve_triangular(lower_factor, slab_values.T, lower=True)  40.3 us
    another operation x20, local copies, waits for them, and re-layouts  11.1 us
  transfers between devices with their start and end apart: 3, of which 2 were waited for; matrix products, arithmetic and copies ran while one was open for 33% of the time, Pallas kernels for 0%

commit v1 on v0

v1 whole, which is shorter than its diff:
```python
import jax
import jax.numpy as jnp
from jax import lax
from jax.sharding import PartitionSpec as P


B = 512
ridge_value = 40.0
HALVES = 2
DEPTH_CHUNKS = 4
GRAM_SLOT = 2


def exact(a, b, dims):
    return lax.dot_general(
        a, b, (dims, ((), ())), precision=lax.Precision.HIGHEST, preferred_element_type=jnp.float32
    )


def times_rows(block, rows):
    return lax.dot_general(
        block,
        rows,
        (((1,), (1,)), ((), ())),
        precision=lax.Precision.HIGH,
        preferred_element_type=jnp.float32,
    )


def kernel(points, anchors):
    feature_count = points.shape[1]
    products = exact(points, anchors, ((1,), (1,)))
    norm_points = jnp.sum(points * points, axis=1)
    norm_anchors = jnp.sum(anchors * anchors, axis=1)
    distance = norm_points[:, None] + norm_anchors[None, :] - 2.0 * products
    return products / feature_count + jnp.exp(-distance / (2.0 * feature_count))


def swapped(x, bit, count):
    return lax.ppermute(x, "col", [(i, i ^ bit) for i in range(count)])


def reduce_rows(x):
    count = lax.axis_size("col")
    index = lax.axis_index("col")
    x = x.reshape(count, x.shape[0] // count, x.shape[1])
    bit = 1
    while bit < count:
        pairs = x.reshape(x.shape[0] // 2, 2, *x.shape[1:])
        upper = (index & bit) != 0
        kept = jnp.where(upper, pairs[:, 1], pairs[:, 0])
        sent = jnp.where(upper, pairs[:, 0], pairs[:, 1])
        got = swapped(sent, bit, count)
        x = kept + got
        bit *= 2
    return x[0]


def gather_rows(x):
    count = lax.axis_size("col")
    index = lax.axis_index("col")
    x = x[None]
    bit = count // 2
    while bit >= 1:
        got = swapped(x, bit, count)
        upper = (index & bit) != 0
        x = jnp.stack([jnp.where(upper, got, x), jnp.where(upper, x, got)], axis=1)
        x = x.reshape(x.shape[0] * 2, *x.shape[2:])
        bit //= 2
    return x.reshape(x.shape[0] * x.shape[1], x.shape[2])


def ladder(rows):
    length = rows // 2
    along = [(0, 2 * (length - 1))]
    along += [(2 * z, 2 * (z - 1)) for z in range(length - 1, 1, -1)]
    along += [(2 * z + 1, 2 * z + 3) for z in range(length - 1)]
    along += [(2 * length - 1, 1)]
    across = [(0, 1)]
    across += [(2 * z + x, 2 * z + 1 - x) for z in range(1, length) for x in (0, 1)]
    return along, across


def on_device(features, factor):
    rows_dev, depth = factor.shape
    row_count = lax.axis_size("row")
    col_count = lax.axis_size("col")
    col_index = lax.axis_index("col")
    row_index = lax.axis_index("row")
    slab_rows = rows_dev // col_count
    length = row_count // 2
    z, x = row_index // 2, row_index % 2
    is_source = row_index == 0
    along, across = ladder(row_count)
    chunks = HALVES * DEPTH_CHUNKS
    wide, deep = B // HALVES, depth // DEPTH_CHUNKS

    own = factor[:B]
    pieces = []
    for u in range(chunks):
        half, part = divmod(u, DEPTH_CHUNKS)
        pieces.append(own[half * wide : (half + 1) * wide, part * deep : (part + 1) * deep])
    a_own = [p[:, : deep // 2] for p in pieces]
    b_own = [p[:, deep // 2 :] for p in pieces]

    gram = times_rows(own, own)
    gram = reduce_rows(gram)
    share = B // col_count
    points_share = lax.dynamic_slice_in_dim(features, col_index * share, share, 1).T
    feature_count = points_share.shape[1]
    extra = jnp.concatenate(
        [gram, jnp.pad(points_share, ((0, 0), (0, B // 2 - feature_count)))], axis=1
    )
    flat = jnp.pad(extra, ((0, 0), (0, wide * deep // 2 // share - extra.shape[1])))
    spare_shape = flat.shape
    spare = flat.reshape(share * (spare_shape[1] // (deep // 2)), deep // 2)
    b_own.insert(GRAM_SLOT, spare)

    def staged(t, spare, factor):
        slots = list(range(chunks))
        slots.insert(GRAM_SLOT, None)
        pair = []
        for u, part in ((min(t, chunks - 1), 0), (slots[min(t, chunks)], 1)):
            if u is None:
                pair.append(spare)
                continue
            half, k = divmod(u, DEPTH_CHUNKS)
            at = k * deep + part * (deep // 2)
            p = factor[half * wide : (half + 1) * wide, at : at + deep // 2]
            pair.append(jnp.where(is_source, p, jnp.zeros_like(p)))
        return lax.optimization_barrier(tuple(pair))

    along_got, across_got = [], []
    relays_across = (x == 1) & ((z == 0) | (z == length - 1))

    def pick(options, default):
        for condition, value in options:
            default = jnp.where(condition, value, default)
        return default

    def chunk_a(u):
        options = [((x == 0) & (z == k), across_got[u + k + 1]) for k in range(1, length - 1)]
        options += [((x == 1) & (z == k), along_got[u + k]) for k in range(1, length)]
        options += [((x == 1) & (z == 0), across_got[u]), (is_source, a_own[u])]
        return pick(options, across_got[u + length])

    def chunk_b(u):
        options = [((x == 0) & (z == k), along_got[u + length - 1 - k]) for k in range(1, length - 1)]
        options += [((x == 1) & (z == k), across_got[u + length - k]) for k in range(1, length)]
        options += [((x == 1) & (z == 0), along_got[u + 2]), (is_source, b_own[u])]
        return pick(options, along_got[u])

    sums = [None] * HALVES
    reduced_sums = [None] * HALVES

    def update(u, factor):
        half, part = divmod(u, DEPTH_CHUNKS)
        chunk = [chunk_a(u), chunk_b(u if u < GRAM_SLOT else u + 1)]
        chunk = lax.optimization_barrier(jnp.concatenate(chunk, axis=1))
        product = times_rows(factor[:, part * deep : (part + 1) * deep], chunk)
        sums[half] = lax.optimization_barrier(product if part == 0 else sums[half] + product)
        if part == DEPTH_CHUNKS - 1:
            reduced_sums[half] = reduce_rows(sums[half])

    staged_next = staged(0, spare, factor)
    for t in range(chunks + length):
        next_a, next_b = staged_next
        if t == 0:
            send_along, send_across = next_b, next_a
        else:
            send_along = jnp.where(relays_across, across_got[-1], along_got[-1])
            send_across = along_got[-1]
            if t <= chunks:
                send_along = jnp.where(is_source, next_b, send_along)
            if t < chunks:
                send_across = jnp.where(is_source, next_a, send_across)
        send_along, send_across, spare, factor, along_got, across_got = lax.optimization_barrier(
            (send_along, send_across, spare, factor, along_got, across_got)
        )
        if t < chunks:
            staged_next = staged(t + 1, spare, factor)
        u = t - length - 1
        if u >= 0:
            update(u, factor)
        if t < chunks + length - 1:
            got_along = lax.ppermute(send_along, "row", along)
        got_across = lax.ppermute(send_across, "row", across)
        along_got = [*along_got, got_along]
        across_got = [*across_got, got_across]

        slot = t - (length - 1)
        if slot == GRAM_SLOT:
            extra = chunk_b(slot).reshape(spare_shape)[:, : B + B // 2]
            everything = gather_rows(extra)
            gram_all = everything[:, :B]
            panel_points = everything[:, B : B + feature_count]
            pivot_kernel = kernel(panel_points, panel_points)
            pivot = pivot_kernel + ridge_value * jnp.eye(B, dtype=jnp.float32) - gram_all
            lower = jnp.linalg.cholesky(pivot)
            inverse = jax.scipy.linalg.solve_triangular(
                lower, jnp.eye(B, dtype=jnp.float32), lower=True
            )
            own_points = lax.dynamic_slice_in_dim(
                features, col_index * slab_rows, slab_rows, 1
            ).T
            global_rows = (
                row_index * rows_dev + col_index * slab_rows + lax.iota(jnp.int32, slab_rows)
            )
            diagonal = global_rows[:, None] == lax.iota(jnp.int32, B)[None, :]
            slab = kernel(own_points, panel_points) + ridge_value * diagonal.astype(jnp.float32)
    update(chunks - 1, factor)

    result = None
    for half in range(HALVES):
        columns = slice(half * wide, (half + 1) * wide)
        part = exact(slab[:, columns] - reduced_sums[half], inverse[:, columns], ((1,), (1,)))
        result = part if result is None else result + part
    return result


def solution(mesh):
    placed = (P(None, "row"), P("row", "col"))
    return jax.shard_map(
        on_device, mesh=mesh, in_specs=placed, out_specs=P(("row", "col"), None), check_vma=False
    )
```

time: 510 us -> 445 us (0.87)
  waiting for transfers between devices: 285 us -> 69.8 us
  starting transfers between devices: 0.09 us -> 97.5 us
  other arithmetic: 128 us -> 172 us
  local copies, waits for them, and re-layouts: 13.1 us -> 32.7 us
  between operations: 16.5 us -> 4.02 us
    psum x2 -> x0, waiting for transfers between devices: 285 us -> none  [the longest x1 281 us: broadcast(): return lax.psum(jnp.where(mine, x, jnp.zeros_like(x)), axis)]
    ppermute x0 -> x31, starting transfers between devices: none -> 97.5 us  [the longest x11 50.6 us: on_device(): got_along = lax.ppermute(send_along, 'row', along)]
    ppermute x0 -> x31, waiting for transfers between devices: none -> 69.8 us  [the longest x11 29.3 us: on_device(): got_along = lax.ppermute(send_along, 'row', along)]
    select_n x2 -> x35, other arithmetic: 8.44 us -> 37.9 us  [the longest x8 15.4 us: pick(): default = jnp.where(condition, value, default)]
    another operation x13, matrix products: 5.37 us -> 17 us  [the longest x7 8.55 us: on_device(): jax.scipy.linalg.solve_triangular(lower, jnp.eye(B, dtype=jnp.float32), l...]
    another operation x34 -> x35, local copies, waits for them, and re-layouts: 11.8 us -> 22.9 us
    dot_general x4 -> x13, matrix products: 53.2 us -> 43.4 us  [the longest x9 35.6 us: times_rows(): lax.dot_general(block, rows, (((1,), (1,)), ((), ())), precision=lax.Prec...]
    another operation x17 -> x19, other arithmetic: 119 us -> 125 us  [the longest x14 78.9 us: on_device(): lower = jnp.linalg.cholesky(pivot)]
  transfers between devices with their start and end apart: 3 -> 31, of which waited for: 2 -> 20; matrix products, arithmetic and copies ran while one was open for 33% -> 55% of each run, Pallas kernels for 0% -> 0%
where the time goes in v1:
time: 445 us; the launch traced here: 437 us
  other arithmetic  172 us (39%)
  starting transfers between devices  97.5 us (22%)
  waiting for transfers between devices  69.8 us (16%)
  matrix products  60.4 us (14%)
  local copies, waits for them, and re-layouts  32.7 us (7%)
    another operation x14, other arithmetic, on_device(): lower = jnp.linalg.cholesky(pivot)  78.9 us
    ppermute x11, starting transfers between devices, on_device(): got_along = lax.ppermute(send_along, 'row', along)  50.6 us
    another operation x4, other arithmetic, on_device(): jax.scipy.linalg.solve_triangular(lower, jnp.eye(B, dtype=jnp.float32), l...  43.1 us
    ppermute x12, starting transfers between devices, on_device(): got_across = lax.ppermute(send_across, 'row', across)  39.5 us
    dot_general x9, matrix products, times_rows(): lax.dot_general(block, rows, (((1,), (1,)), ((), ())), precision=lax.Prec...  35.6 us
    ppermute x11, waiting for transfers between devices, on_device(): got_along = lax.ppermute(send_along, 'row', along)  29.3 us
    ppermute x12, waiting for transfers between devices, on_device(): got_across = lax.ppermute(send_across, 'row', across)  25 us
    ppermute x8, waiting for transfers between devices, swapped(): return lax.ppermute(x, 'col', [(i, i ^ bit) for i in range(count)])  15.4 us
  transfers between devices with their start and end apart: 31, of which 20 were waited for; matrix products, arithmetic and copies ran while one was open for 55% of the time, Pallas kernels for 0%

profile of v1, /device:TPU:0, one launch (start us, length us, event | category | flops | bytes accessed | tf_op | source)
XLA Modules:
  0.0 436.7 jit_solution(16110971371927043987)
XLA Ops:
  0.0 10.4 %fusion = f32[512,512]{1,0:T(8,128)S(1)} fusion(f32[1024,4096]{1,0:T(8,128)} %param.3), kind=kOutput, calls=%fused_computation.2 | convolution fusion | flops 6442450944 | bytes 9437184 | tf_op jit(solution)/shard_map/dot_general | solution.py:21
  17.8 4.5 %collective-permute-done.1 = f32[1,128,512]{2,1,0:T(8,128)S(1)} collective-permute-done((f32[1,128,512]{2,1,0:T(8,128)S(1)}, f32[1,128,512]{2,1,0:T(8,128)S(1)}, u32[]{:S(2)}, u32[]{:S(2)}) %collective-permute-start.1) | collective-permute-done | bytes 262176 | tf_op jit(solution)/shard_map/ppermute | solution.py:40
  26.3 5.5 %collective-permute-start.3 = (f32[256,512]{1,0:T(8,128)S(1)}, f32[256,512]{1,0:T(8,128)S(1)}, u32[]{:S(2)}, u32[]{:S(2)}) collective-permute-start(f32[256,512]{1,0:T(8,128)S(1)} %get-tuple-element.148), channel_id=1, source_target_pairs={{0,24},{24,16},{16,8},{4,12},{12,20},{20,28},{28,4},{1,25},{25,17}... | collective-permute-start | bytes 1572872 | tf_op jit(solution)/shard_map/ppermute | solution.py:186
  37.1 4.9 %collective-permute-done.3 = f32[256,512]{1,0:T(8,128)S(1)} collective-permute-done((f32[256,512]{1,0:T(8,128)S(1)}, f32[256,512]{1,0:T(8,128)S(1)}, u32[]{:S(2)}, u32[]{:S(2)}) %collective-permute-start.3) | collective-permute-done | bytes 524320 | tf_op jit(solution)/shard_map/ppermute | solution.py:186
  45.5 4.9 %collective-permute-start.5 = (f32[256,512]{1,0:T(8,128)S(1)}, f32[256,512]{1,0:T(8,128)S(1)}, u32[]{:S(2)}, u32[]{:S(2)}) collective-permute-start(f32[256,512]{1,0:T(8,128)S(1)} %get-tuple-element.155), channel_id=1, source_target_pairs={{0,24},{24,16},{16,8},{4,12},{12,20},{20,28},{28,4},{1,25},{25,17}... | collective-permute-start | bytes 1572872 | tf_op jit(solution)/shard_map/ppermute | solution.py:186
  55.2 4.7 %collective-permute-done.5 = f32[256,512]{1,0:T(8,128)S(1)} collective-permute-done((f32[256,512]{1,0:T(8,128)S(1)}, f32[256,512]{1,0:T(8,128)S(1)}, u32[]{:S(2)}, u32[]{:S(2)}) %collective-permute-start.5) | collective-permute-done | bytes 524320 | tf_op jit(solution)/shard_map/ppermute | solution.py:186
  60.1 4.4 %collective-permute-start.6 = (f32[256,512]{1,0:T(8,128)S(1)}, f32[256,512]{1,0:T(8,128)S(1)}, u32[]{:S(2)}, u32[]{:S(2)}) collective-permute-start(f32[256,512]{1,0:T(8,128)S(1)} %get-tuple-element.161), channel_id=1, source_target_pairs={{0,4},{8,12},{12,8},{16,20},{20,16},{24,28},{28,24},{1,5},{9,13},{... | collective-permute-start | bytes 1572872 | tf_op jit(solution)/shard_map/ppermute | solution.py:187
  78.1 4.4 %collective-permute-start.8 = (f32[256,512]{1,0:T(8,128)}, f32[256,512]{1,0:T(8,128)S(1)}, u32[]{:S(2)}, u32[]{:S(2)}) collective-permute-start(f32[256,512]{1,0:T(8,128)} %get-tuple-element.170), channel_id=1, source_target_pairs={{0,4},{8,12},{12,8},{16,20},{20,16},{24,28},{28,24},{1,5},{9,13},{... | collective-permute-start | bytes 1572872 | tf_op jit(solution)/shard_map/ppermute | solution.py:187
  95.5 4.3 collective-permute-start.10
  111.0 4.4 %collective-permute-start.12 = (f32[256,512]{1,0:T(8,128)S(1)}, f32[256,512]{1,0:T(8,128)S(1)}, u32[]{:S(2)}, u32[]{:S(2)}) collective-permute-start(f32[256,512]{1,0:T(8,128)S(1)} %get-tuple-element.195), channel_id=1, source_target_pairs={{0,4},{8,12},{12,8},{16,20},{20,16},{24,28},{28,24},{1,5},{9,13},{... | collective-permute-start | bytes 1572872 | tf_op jit(solution)/shard_map/ppermute | solution.py:187
  122.3 5.1 %fusion.16 = f32[1024,256]{1,0:T(8,128)} fusion(f32[256,1024]{1,0:T(8,128)S(1)} %pad_maximum_fusion.1, f32[1024,4096]{1,0:T(8,128)} %param.3), kind=kOutput, calls=%fused_computation.18 | convolution fusion | flops 1610612736 | bytes 6291456 | tf_op jit(solution)/shard_map/dot_general | solution.py:21
  137.6 4.5 %collective-permute-start.17 = (f32[256,512]{1,0:T(8,128)}, f32[256,512]{1,0:T(8,128)S(1)}, u32[]{:S(2)}, u32[]{:S(2)}) collective-permute-start(f32[256,512]{1,0:T(8,128)} %get-tuple-element.219), channel_id=1, source_target_pairs={{0,24},{24,16},{16,8},{4,12},{12,20},{20,28},{28,4},{1,25},{25,17}... | collective-permute-start | bytes 1572872 | tf_op jit(solution)/shard_map/ppermute | solution.py:186
  144.5 4.2 fusion.14
  154.3 5.2 %collective-permute-start.19 = (f32[256,512]{1,0:T(8,128)S(1)}, f32[256,512]{1,0:T(8,128)}, u32[]{:S(2)}, u32[]{:S(2)}) collective-permute-start(f32[256,512]{1,0:T(8,128)S(1)} %get-tuple-element.231), channel_id=1, source_target_pairs={{0,24},{24,16},{16,8},{4,12},{12,20},{20,28},{28,4},{1,25},{25,17}... | collective-permute-start | bytes 1572872 | tf_op jit(solution)/shard_map/ppermute | solution.py:186
  172.2 4.3 collective-permute-start.22
  176.4 4.9 %collective-permute-start.23 = (f32[256,512]{1,0:T(8,128)}, f32[256,512]{1,0:T(8,128)}, u32[]{:S(2)}, u32[]{:S(2)}) collective-permute-start(f32[256,512]{1,0:T(8,128)} %select_select_fusion.11), channel_id=1, source_target_pairs={{0,24},{24,16},{16,8},{4,12},{12,20},{20,28},{28,4},{1,25},{25,17}... | collective-permute-start | bytes 1572872 | tf_op jit(solution)/shard_map/ppermute | solution.py:186
  202.3 11.7 %cholesky.103 = f32[128,128]{1,0:T(8,128)S(1)} custom-call(f32[128,128]{1,0:T(8,128)S(1)} %cholesky.263), custom_call_target="Cholesky" | custom-call | tf_op jit(solution)/shard_map/jit(cholesky)/cholesky | solution.py:199
  214.8 9.8 %custom-call.31 = f32[1,128,128]{1,2,0:T(8,128)S(1)} custom-call(f32[1,128,128]{2,1,0:T(8,128)S(1)} %get-tuple-element.361), custom_call_target="InvertDiagBlocksLowerTriangular" | custom-call | tf_op jit(solution)/shard_map/jit(cholesky)/cholesky | solution.py:199
  228.7 12.1 %cholesky.215 = f32[128,128]{1,0:T(8,128)S(1)} custom-call(f32[128,128]{1,0:T(8,128)S(1)} %cholesky.267), custom_call_target="Cholesky" | custom-call | tf_op jit(solution)/shard_map/jit(cholesky)/cholesky | solution.py:199
  240.9 9.8 %custom-call.32 = f32[1,128,128]{1,2,0:T(8,128)S(1)} custom-call(f32[1,128,128]{2,1,0:T(8,128)S(1)} %get-tuple-element.359), custom_call_target="InvertDiagBlocksLowerTriangular" | custom-call | tf_op jit(solution)/shard_map/jit(cholesky)/cholesky | solution.py:199
  255.5 11.7 %cholesky.236 = f32[128,128]{1,0:T(8,128)S(1)} custom-call(f32[128,128]{1,0:T(8,128)S(1)} %cholesky.272), custom_call_target="Cholesky" | custom-call | tf_op jit(solution)/shard_map/jit(cholesky)/cholesky | solution.py:199
  268.0 9.8 %custom-call.33 = f32[1,128,128]{1,2,0:T(8,128)S(1)} custom-call(f32[1,128,128]{2,1,0:T(8,128)S(1)} %get-tuple-element.357), custom_call_target="InvertDiagBlocksLowerTriangular" | custom-call | tf_op jit(solution)/shard_map/jit(cholesky)/cholesky | solution.py:199
  280.3 11.9 %cholesky.253 = f32[128,128]{1,0:T(8,128)S(1)} custom-call(f32[128,128]{1,0:T(8,128)S(1)} %convolution_subtract_fusion.5), custom_call_target="Cholesky" | custom-call | tf_op jit(solution)/shard_map/jit(cholesky)/cholesky | solution.py:199
  300.5 14.6 %while.1 = (s32[]{:T(128)}, f32[512,512]{0,1:T(8,128)}, s32[4,2]{0,1:T(2,128)S(1)}, f32[4,128,128]{2,1,0:T(8,128)}, s32[]{:T(128)}) while((s32[]{:T(128)}, f32[512,512]{0,1:T(8,128)}, s32[4,2]{0,1:T(2,128)S(1)}, f32[4,128,128]{2,1,0:T(8,128)}, s32[]{:T(128)}) %tuple.100), condition=%wide.while_cond, body=%wide.while_body.sunk | while | flops 2 | bytes 393329 | solution.py:200
  315.1 40.1 %custom-call.34 = f32[4,128,128]{1,2,0:T(8,128)S(1)} custom-call(f32[4,128,128]{2,1,0:T(8,128)} %get-tuple-element.288), custom_call_target="InvertDiagBlocksLowerTriangular" | custom-call | tf_op jit(solution)/shard_map/jit(_solve_triangular)/triangular_solve | solution.py:200
  372.5 4.2 fusion.8
  381.6 6.5 %collective-permute-start.26 = (f32[256,512]{1,0:T(8,128)S(1)}, f32[256,512]{1,0:T(8,128)S(1)}, u32[]{:S(2)}, u32[]{:S(2)}) collective-permute-start(f32[256,512]{1,0:T(8,128)S(1)} %broadcast_select_fusion.2), channel_id=1, source_target_pairs={{0,24},{24,16},{16,8},{4,12},{12,20},{20,28},{28,4},{1,25},{25,17}... | collective-permute-start | bytes 1572872 | tf_op jit(solution)/shard_map/ppermute | solution.py:186
  391.9 4.2 fusion.6
  400.0 4.4 %collective-permute-start.28 = (f32[256,512]{1,0:T(8,128)S(1)}, f32[256,512]{1,0:T(8,128)S(1)}, u32[]{:S(2)}, u32[]{:S(2)}) collective-permute-start(f32[256,512]{1,0:T(8,128)S(1)} %collective-permute-done.26), channel_id=1, source_target_pairs={{0,4},{8,12},{12,8},{16,20},{20,16},{24,28},{28,24},{1,5},{9,13},{... | collective-permute-start | bytes 1572872 | tf_op jit(solution)/shard_map/ppermute | solution.py:187
  408.4 5.8 %collective-permute-done.28 = f32[256,512]{1,0:T(8,128)S(1)} collective-permute-done((f32[256,512]{1,0:T(8,128)S(1)}, f32[256,512]{1,0:T(8,128)S(1)}, u32[]{:S(2)}, u32[]{:S(2)}) %collective-permute-start.28) | collective-permute-done | bytes 524320 | tf_op jit(solution)/shard_map/ppermute | solution.py:187
  424.0 5.9 %collective-permute-done.30 = f32[1,256,256]{2,1,0:T(8,128)S(1)} collective-permute-done((f32[1,256,256]{2,1,0:T(8,128)S(1)}, f32[1,256,256]{2,1,0:T(8,128)S(1)}, u32[]{:S(2)}, u32[]{:S(2)}) %collective-permute-start.30) | collective-permute-done | bytes 262176 | tf_op jit(solution)/shard_map/ppermute | solution.py:40
  430.6 4.5 %collective-permute-done.21 = f32[1,256,256]{2,1,0:T(8,128)S(1)} collective-permute-done((f32[1,256,256]{2,1,0:T(8,128)S(1)}, f32[1,256,256]{2,1,0:T(8,128)S(1)}, u32[]{:S(2)}, u32[]{:S(2)}) %collective-permute-start.21) | collective-permute-done | bytes 262176 | tf_op jit(solution)/shard_map/ppermute | solution.py:40
  (239 shorter events, 199.7 us)
Async XLA Ops:
  10.5 2.1 collective-permute-start
  12.8 9.5 %collective-permute-start.1 = (f32[1,128,512]{2,1,0:T(8,128)S(1)}, f32[1,128,512]{2,1,0:T(8,128)S(1)}, u32[]{:S(2)}, u32[]{:S(2)}) collective-permute-start(f32[1,128,512]{2,1,0:T(8,128)S(1)} %select_bitcast_fusion.5), channel_id=1, source_target_pairs={{0,2},{1,3},{2,0},{3,1},{4,6},{5,7},{6,4},{7,5},{8,10},{9,11},{10,... | collective-permute-start | bytes 786440 | tf_op jit(solution)/shard_map/ppermute | solution.py:40
  22.6 14.6 %collective-permute-start.2 = (f32[256,512]{1,0:T(8,128)}, f32[256,512]{1,0:T(8,128)S(1)}, u32[]{:S(2)}, u32[]{:S(2)}) collective-permute-start(f32[256,512]{1,0:T(8,128)} %get-tuple-element.147), channel_id=1, source_target_pairs={{0,4},{8,12},{12,8},{16,20},{20,16},{24,28},{28,24},{1,5},{9,13},{... | collective-permute-start | bytes 1572872 | tf_op jit(solution)/shard_map/ppermute | solution.py:187
  26.3 15.8 %collective-permute-start.3 = (f32[256,512]{1,0:T(8,128)S(1)}, f32[256,512]{1,0:T(8,128)S(1)}, u32[]{:S(2)}, u32[]{:S(2)}) collective-permute-start(f32[256,512]{1,0:T(8,128)S(1)} %get-tuple-element.148), channel_id=1, source_target_pairs={{0,24},{24,16},{16,8},{4,12},{12,20},{20,28},{28,4},{1,25},{25,17}... | collective-permute-start | bytes 1572872 | tf_op jit(solution)/shard_map/ppermute | solution.py:186
  42.3 12.9 %collective-permute-start.4 = (f32[256,512]{1,0:T(8,128)S(1)}, f32[256,512]{1,0:T(8,128)S(1)}, u32[]{:S(2)}, u32[]{:S(2)}) collective-permute-start(f32[256,512]{1,0:T(8,128)S(1)} %get-tuple-element.154), channel_id=1, source_target_pairs={{0,4},{8,12},{12,8},{16,20},{20,16},{24,28},{28,24},{1,5},{9,13},{... | collective-permute-start | bytes 1572872 | tf_op jit(solution)/shard_map/ppermute | solution.py:187
  45.5 14.4 %collective-permute-start.5 = (f32[256,512]{1,0:T(8,128)S(1)}, f32[256,512]{1,0:T(8,128)S(1)}, u32[]{:S(2)}, u32[]{:S(2)}) collective-permute-start(f32[256,512]{1,0:T(8,128)S(1)} %get-tuple-element.155), channel_id=1, source_target_pairs={{0,24},{24,16},{16,8},{4,12},{12,20},{20,28},{28,4},{1,25},{25,17}... | collective-permute-start | bytes 1572872 | tf_op jit(solution)/shard_map/ppermute | solution.py:186
  59.9 51.1 %copy-start.14 = (f32[256,512]{1,0:T(8,128)}, f32[256,512]{1,0:T(8,128)S(1)}, u32[]{:S(2)}) copy-start(f32[256,512]{1,0:T(8,128)S(1)} %collective-permute-done.5) | copy-start | bytes 1572868
  60.1 13.0 %collective-permute-start.6 = (f32[256,512]{1,0:T(8,128)S(1)}, f32[256,512]{1,0:T(8,128)S(1)}, u32[]{:S(2)}, u32[]{:S(2)}) collective-permute-start(f32[256,512]{1,0:T(8,128)S(1)} %get-tuple-element.161), channel_id=1, source_target_pairs={{0,4},{8,12},{12,8},{16,20},{20,16},{24,28},{28,24},{1,5},{9,13},{... | collective-permute-start | bytes 1572872 | tf_op jit(solution)/shard_map/ppermute | solution.py:187
  64.6 12.3 %collective-permute-start.7 = (f32[256,512]{1,0:T(8,128)S(1)}, f32[256,512]{1,0:T(8,128)S(1)}, u32[]{:S(2)}, u32[]{:S(2)}) collective-permute-start(f32[256,512]{1,0:T(8,128)S(1)} %get-tuple-element.162), channel_id=1, source_target_pairs={{0,24},{24,16},{16,8},{4,12},{12,20},{20,28},{28,4},{1,25},{25,17}... | collective-permute-start | bytes 1572872 | tf_op jit(solution)/shard_map/ppermute | solution.py:186
  78.1 12.5 %collective-permute-start.8 = (f32[256,512]{1,0:T(8,128)}, f32[256,512]{1,0:T(8,128)S(1)}, u32[]{:S(2)}, u32[]{:S(2)}) collective-permute-start(f32[256,512]{1,0:T(8,128)} %get-tuple-element.170), channel_id=1, source_target_pairs={{0,4},{8,12},{12,8},{16,20},{20,16},{24,28},{28,24},{1,5},{9,13},{... | collective-permute-start | bytes 1572872 | tf_op jit(solution)/shard_map/ppermute | solution.py:187
  82.5 11.8 %collective-permute-start.9 = (f32[256,512]{1,0:T(8,128)}, f32[256,512]{1,0:T(8,128)S(1)}, u32[]{:S(2)}, u32[]{:S(2)}) collective-permute-start(f32[256,512]{1,0:T(8,128)} %get-tuple-element.171), channel_id=1, source_target_pairs={{0,24},{24,16},{16,8},{4,12},{12,20},{20,28},{28,4},{1,25},{25,17}... | collective-permute-start | bytes 1572872 | tf_op jit(solution)/shard_map/ppermute | solution.py:186
  95.5 12.3 %collective-permute-start.10 = (f32[256,512]{1,0:T(8,128)}, f32[256,512]{1,0:T(8,128)S(1)}, u32[]{:S(2)}, u32[]{:S(2)}) collective-permute-start(f32[256,512]{1,0:T(8,128)} %get-tuple-element.181), channel_id=1, source_target_pairs={{0,4},{8,12},{12,8},{16,20},{20,16},{24,28},{28,24},{1,5},{9,13},{... | collective-permute-start | bytes 1572872 | tf_op jit(solution)/shard_map/ppermute | solution.py:187
  99.8 10.9 %collective-permute-start.11 = (f32[256,512]{1,0:T(8,128)}, f32[256,512]{1,0:T(8,128)S(1)}, u32[]{:S(2)}, u32[]{:S(2)}) collective-permute-start(f32[256,512]{1,0:T(8,128)} %get-tuple-element.182), channel_id=1, source_target_pairs={{0,24},{24,16},{16,8},{4,12},{12,20},{20,28},{28,4},{1,25},{25,17}... | collective-permute-start | bytes 1572872 | tf_op jit(solution)/shard_map/ppermute | solution.py:186
  111.0 17.7 %collective-permute-start.12 = (f32[256,512]{1,0:T(8,128)S(1)}, f32[256,512]{1,0:T(8,128)S(1)}, u32[]{:S(2)}, u32[]{:S(2)}) collective-permute-start(f32[256,512]{1,0:T(8,128)S(1)} %get-tuple-element.195), channel_id=1, source_target_pairs={{0,4},{8,12},{12,8},{16,20},{20,16},{24,28},{28,24},{1,5},{9,13},{... | collective-permute-start | bytes 1572872 | tf_op jit(solution)/shard_map/ppermute | solution.py:187
  115.4 13.2 %collective-permute-start.15 = (f32[256,512]{1,0:T(8,128)S(1)}, f32[256,512]{1,0:T(8,128)S(1)}, u32[]{:S(2)}, u32[]{:S(2)}) collective-permute-start(f32[256,512]{1,0:T(8,128)S(1)} %get-tuple-element.205), channel_id=1, source_target_pairs={{0,24},{24,16},{16,8},{4,12},{12,20},{20,28},{28,4},{1,25},{25,17}... | collective-permute-start | bytes 1572872 | tf_op jit(solution)/shard_map/ppermute | solution.py:186
  134.4 15.8 %collective-permute-start.13 = (f32[1,128,768]{1,2,0:T(8,128)}, f32[1,128,768]{1,2,0:T(8,128)S(1)}, u32[]{:S(2)}, u32[]{:S(2)}) collective-permute-start(f32[1,128,768]{1,2,0:T(8,128)} %bitcast.190), channel_id=1, source_target_pairs={{0,2},{1,3},{2,0},{3,1},{4,6},{5,7},{6,4},{7,5},{8,10},{9,11},{10,... | collective-permute-start | bytes 1179656 | tf_op jit(solution)/shard_map/ppermute | solution.py:40
  136.0 15.1 %collective-permute-start.16 = (f32[256,512]{1,0:T(8,128)}, f32[256,512]{1,0:T(8,128)S(1)}, u32[]{:S(2)}, u32[]{:S(2)}) collective-permute-start(f32[256,512]{1,0:T(8,128)} %get-tuple-element.218), channel_id=1, source_target_pairs={{0,4},{8,12},{12,8},{16,20},{20,16},{24,28},{28,24},{1,5},{9,13},{... | collective-permute-start | bytes 1572872 | tf_op jit(solution)/shard_map/ppermute | solution.py:187
  137.6 13.5 %collective-permute-start.17 = (f32[256,512]{1,0:T(8,128)}, f32[256,512]{1,0:T(8,128)S(1)}, u32[]{:S(2)}, u32[]{:S(2)}) collective-permute-start(f32[256,512]{1,0:T(8,128)} %get-tuple-element.219), channel_id=1, source_target_pairs={{0,24},{24,16},{16,8},{4,12},{12,20},{20,28},{28,4},{1,25},{25,17}... | collective-permute-start | bytes 1572872 | tf_op jit(solution)/shard_map/ppermute | solution.py:186
  151.0 33.9 %collective-permute-start.14 = (f32[2,128,768]{1,0,2:T(2,128)S(1)}, f32[2,128,768]{1,0,2:T(2,128)S(1)}, u32[]{:S(2)}, u32[]{:S(2)}) collective-permute-start(f32[2,128,768]{1,0,2:T(2,128)S(1)} %maximum_bitcast_fusion), channel_id=1, source_target_pairs={{0,1},{1,0},{2,3},{3,2},{4,5},{5,4},{6,7},{7,6},{8,9},{9,8},{10,11... | collective-permute-start | bytes 2359304 | tf_op jit(solution)/shard_map/ppermute | solution.py:40
  152.6 13.5 %collective-permute-start.18 = (f32[256,512]{1,0:T(8,128)S(1)}, f32[256,512]{1,0:T(8,128)S(1)}, u32[]{:S(2)}, u32[]{:S(2)}) collective-permute-start(f32[256,512]{1,0:T(8,128)S(1)} %get-tuple-element.230), channel_id=1, source_target_pairs={{0,4},{8,12},{12,8},{16,20},{20,16},{24,28},{28,24},{1,5},{9,13},{... | collective-permute-start | bytes 1572872 | tf_op jit(solution)/shard_map/ppermute | solution.py:187
  154.3 15.9 %collective-permute-start.19 = (f32[256,512]{1,0:T(8,128)S(1)}, f32[256,512]{1,0:T(8,128)}, u32[]{:S(2)}, u32[]{:S(2)}) collective-permute-start(f32[256,512]{1,0:T(8,128)S(1)} %get-tuple-element.231), channel_id=1, source_target_pairs={{0,24},{24,16},{16,8},{4,12},{12,20},{20,28},{28,4},{1,25},{25,17}... | collective-permute-start | bytes 1572872 | tf_op jit(solution)/shard_map/ppermute | solution.py:186
  172.2 191.2 %collective-permute-start.22 = (f32[256,512]{1,0:T(8,128)}, f32[256,512]{1,0:T(8,128)}, u32[]{:S(2)}, u32[]{:S(2)}) collective-permute-start(f32[256,512]{1,0:T(8,128)} %collective-permute-done.19), channel_id=1, source_target_pairs={{0,4},{8,12},{12,8},{16,20},{20,16},{24,28},{28,24},{1,5},{9,13},{... | collective-permute-start | bytes 1572872 | tf_op jit(solution)/shard_map/ppermute | solution.py:187
  176.4 187.0 %collective-permute-start.23 = (f32[256,512]{1,0:T(8,128)}, f32[256,512]{1,0:T(8,128)}, u32[]{:S(2)}, u32[]{:S(2)}) collective-permute-start(f32[256,512]{1,0:T(8,128)} %select_select_fusion.11), channel_id=1, source_target_pairs={{0,24},{24,16},{16,8},{4,12},{12,20},{20,28},{28,4},{1,25},{25,17}... | collective-permute-start | bytes 1572872 | tf_op jit(solution)/shard_map/ppermute | solution.py:186
  184.9 236.5 %collective-permute-start.20 = (f32[2,256,256]{2,1,0:T(8,128)}, f32[2,256,256]{2,1,0:T(8,128)}, u32[]{:S(2)}, u32[]{:S(2)}) collective-permute-start(f32[2,256,256]{2,1,0:T(8,128)} %select_bitcast_fusion.1), channel_id=1, source_target_pairs={{0,1},{1,0},{2,3},{3,2},{4,5},{5,4},{6,7},{7,6},{8,9},{9,8},{10,11... | collective-permute-start | bytes 1572872 | tf_op jit(solution)/shard_map/ppermute | solution.py:40
  364.6 14.0 %collective-permute-start.24 = (f32[256,512]{1,0:T(8,128)}, f32[256,512]{1,0:T(8,128)S(1)}, u32[]{:S(2)}, u32[]{:S(2)}) collective-permute-start(f32[256,512]{1,0:T(8,128)} %collective-permute-done.23), channel_id=1, source_target_pairs={{0,4},{8,12},{12,8},{16,20},{20,16},{24,28},{28,24},{1,5},{9,13},{... | collective-permute-start | bytes 1572872 | tf_op jit(solution)/shard_map/ppermute | solution.py:187
  366.2 15.3 %collective-permute-start.25 = (f32[256,512]{1,0:T(8,128)S(1)}, f32[256,512]{1,0:T(8,128)S(1)}, u32[]{:S(2)}, u32[]{:S(2)}) collective-permute-start(f32[256,512]{1,0:T(8,128)S(1)} %broadcast_select_fusion.3), channel_id=1, source_target_pairs={{0,24},{24,16},{16,8},{4,12},{12,20},{20,28},{28,4},{1,25},{25,17}... | collective-permute-start | bytes 1572872 | tf_op jit(solution)/shard_map/ppermute | solution.py:186
  381.6 17.1 %collective-permute-start.26 = (f32[256,512]{1,0:T(8,128)S(1)}, f32[256,512]{1,0:T(8,128)S(1)}, u32[]{:S(2)}, u32[]{:S(2)}) collective-permute-start(f32[256,512]{1,0:T(8,128)S(1)} %broadcast_select_fusion.2), channel_id=1, source_target_pairs={{0,24},{24,16},{16,8},{4,12},{12,20},{20,28},{28,4},{1,25},{25,17}... | collective-permute-start | bytes 1572872 | tf_op jit(solution)/shard_map/ppermute | solution.py:186
  388.0 12.0 %collective-permute-start.27 = (f32[256,512]{1,0:T(8,128)S(1)}, f32[256,512]{1,0:T(8,128)S(1)}, u32[]{:S(2)}, u32[]{:S(2)}) collective-permute-start(f32[256,512]{1,0:T(8,128)S(1)} %collective-permute-done.25), channel_id=1, source_target_pairs={{0,4},{8,12},{12,8},{16,20},{20,16},{24,28},{28,24},{1,5},{9,13},{... | collective-permute-start | bytes 1572872 | tf_op jit(solution)/shard_map/ppermute | solution.py:187
  400.0 14.2 %collective-permute-start.28 = (f32[256,512]{1,0:T(8,128)S(1)}, f32[256,512]{1,0:T(8,128)S(1)}, u32[]{:S(2)}, u32[]{:S(2)}) collective-permute-start(f32[256,512]{1,0:T(8,128)S(1)} %collective-permute-done.26), channel_id=1, source_target_pairs={{0,4},{8,12},{12,8},{16,20},{20,16},{24,28},{28,24},{1,5},{9,13},{... | collective-permute-start | bytes 1572872 | tf_op jit(solution)/shard_map/ppermute | solution.py:187
  418.0 2.5 collective-permute-start.29
  420.7 9.2 %collective-permute-start.30 = (f32[1,256,256]{2,1,0:T(8,128)S(1)}, f32[1,256,256]{2,1,0:T(8,128)S(1)}, u32[]{:S(2)}, u32[]{:S(2)}) collective-permute-start(f32[1,256,256]{2,1,0:T(8,128)S(1)} %select_bitcast_fusion.3), channel_id=1, source_target_pairs={{0,2},{1,3},{2,0},{3,1},{4,6},{5,7},{6,4},{7,5},{8,10},{9,11},{10,... | collective-permute-start | bytes 786440 | tf_op jit(solution)/shard_map/ppermute | solution.py:40
  422.6 12.5 %collective-permute-start.21 = (f32[1,256,256]{2,1,0:T(8,128)S(1)}, f32[1,256,256]{2,1,0:T(8,128)S(1)}, u32[]{:S(2)}, u32[]{:S(2)}) collective-permute-start(f32[1,256,256]{2,1,0:T(8,128)S(1)} %select_bitcast_fusion.4), channel_id=1, source_target_pairs={{0,2},{1,3},{2,0},{3,1},{4,6},{5,7},{6,4},{7,5},{8,10},{9,11},{10,... | collective-permute-start | bytes 786440 | tf_op jit(solution)/shard_map/ppermute | solution.py:40
  (28 other events, 585.4 us)
